TPU v7x, 256 devices: a whole 4x4x8 slice. The times are simulated.
256 devices in a mesh: blk: 32 (over x, z), uly: 8 (over y, core).
Axes of the slice: x: 4, y: 4, z: 8, core: 2. Of those that a mesh axis runs over, the one named last changes fastest.
Arguments:
- tokens: bfloat16 [12288, 3072], P(('blk', 'uly')), may hold values from -6 to 6
- mod_shift: float32 [3072], replicated, may hold values from -3 to 3
- mod_scale: float32 [3072], replicated, may hold values from -2 to 6
- out_gate: float32 [3072], replicated, may hold values from 0.5 to 1.5
- w_qkv: bfloat16 [3072, 24, 384], P(None, 'uly'), may hold values from -0.109375 to 0.109375
- w_out: bfloat16 [3072, 3072], P('uly'), may hold values from -0.109375 to 0.109375
- tile_map: int32 [32], replicated, may hold values from 0 to 31, as said below
- window_corner: int32 [32, 2], replicated, may hold values from 0 to 5, as said below
Outputs:
- mixed: bfloat16 [12288, 3072], P(('blk', 'uly'))
Inputs may be any that keep to these rules, and one draw needn't show every extreme that they name: `tile_map`: A permutation of the tile positions; position j holds a grid tile whose number differs from j by at most 1. `window_corner`: each query tile's 3 x 3 window lies inside the grid and contains the grid tile that its own position holds.
All inputs are finite; a program needn't handle non-finite values.
Results may differ from a plain program's by a relative error of at most 0.02.
The roundings to bfloat16 on the way count: a program that leaves them out, or rounds other values in their place, can miss the bound.
Values may be sent and summed in bfloat16 or wider, within the bound.
A program may use at most 128 MiB of HBM per device.

v0:
```python
import jax
import jax.numpy as jnp
from jax import lax
from jax.sharding import PartitionSpec as P

TILE = 384
WIN = 3
GW = 4


def from_behind(block, axis, distance):
    devices = range(lax.axis_size(axis))
    route = [(i - distance, i) for i in devices if i - distance in devices]
    return lax.ppermute(block, axis, route)


def on_device(tokens, mod_shift, mod_scale, out_gate, w_qkv, w_out, tile_map, window_corner):
    values_in = tokens.astype(jnp.float32)
    mean_row = jnp.mean(values_in, axis=-1, keepdims=True)
    centred = values_in - mean_row
    variance = jnp.mean(centred * centred, axis=-1, keepdims=True)
    normed = (centred * lax.rsqrt(variance + 1e-06) * (1.0 + mod_scale) + mod_shift).astype(
        jnp.bfloat16
    )
    heads_dev = w_qkv.shape[1]
    head_dim = w_qkv.shape[2] // 3
    qkv = jnp.einsum(
        "td,dhe->the",
        lax.all_gather(normed, "uly", axis=0, tiled=True),
        w_qkv,
        preferred_element_type=jnp.float32,
    ).astype(jnp.bfloat16)
    group_rows = qkv.shape[0]
    tiles_here = group_rows // TILE
    all_tiles = tile_map.shape[0]
    queries = qkv[:, :, :head_dim]
    keyval = qkv[:, :, head_dim:]
    shard_idx = lax.axis_index("blk")
    n_blk = lax.axis_size("blk")
    first_tile = shard_idx * tiles_here
    query_corner = lax.dynamic_slice(window_corner, (first_tile, 0), (tiles_here, 2))
    softmax_factor = 1.0 / jnp.sqrt(jnp.float32(head_dim))

    def attend(running, kv_tile, key_tile, is_valid):
        safe_tile = jnp.clip(key_tile, 0, all_tiles - 1)
        key_grid = lax.dynamic_index_in_dim(tile_map, safe_tile, keepdims=False)
        row_gap = key_grid // GW - query_corner[:, 0]
        col_gap = key_grid % GW - query_corner[:, 1]
        inside = (row_gap >= 0) & (row_gap < WIN) & (col_gap >= 0) & (col_gap < WIN) & is_valid

        def compute(state):
            highest, total, accum = state
            row_ok = jnp.repeat(inside, TILE)[None, :, None]
            scores = (
                jnp.einsum(
                    "qhd,khd->hqk",
                    queries,
                    kv_tile[:, :, :head_dim],
                    preferred_element_type=jnp.float32,
                )
                * softmax_factor
            )
            scores = jnp.where(row_ok, scores, -1e30)
            new_high = jnp.maximum(highest, jnp.max(scores, axis=-1))
            probs = jnp.where(row_ok, jnp.exp(scores - new_high[:, :, None]), 0.0)
            factor = jnp.exp(highest - new_high)
            total = total * factor + jnp.sum(probs, axis=-1)
            weights = probs.astype(jnp.bfloat16)
            accum = accum * factor[:, :, None] + jnp.einsum(
                "hqk,khd->hqd",
                weights,
                kv_tile[:, :, head_dim:],
                preferred_element_type=jnp.float32,
            )
            return (new_high, total, accum)

        def keep(state):
            return state

        return lax.cond(jnp.any(inside), compute, keep, running)

    def attend_group(running, arrived, source):
        is_valid = (source >= 0) & (source < n_blk)
        running = attend(running, arrived, source * tiles_here + 0, is_valid)
        return running

    running = (
        jnp.full((heads_dev, group_rows), -1e30, jnp.float32),
        jnp.zeros((heads_dev, group_rows), jnp.float32),
        jnp.zeros((heads_dev, group_rows, head_dim), jnp.float32),
    )
    reach = min((2 * GW + 3 + tiles_here) // tiles_here, n_blk - 1)
    running = attend_group(running, keyval, shard_idx)
    for offset in range(-reach, reach + 1):
        if offset != 0:
            arrived = from_behind(keyval, "blk", offset)
            running = attend_group(running, arrived, shard_idx - offset)
    highest, total, accum = running
    attn = (accum / total[:, :, None]).astype(jnp.bfloat16)
    attn = jnp.transpose(attn, (1, 0, 2)).reshape(group_rows, heads_dev * head_dim)
    summed = lax.psum_scatter(
        jnp.dot(attn, w_out, preferred_element_type=jnp.float32).astype(jnp.bfloat16),
        "uly",
        scatter_dimension=0,
        tiled=True,
    ).astype(jnp.float32)
    return (out_gate * summed).astype(jnp.bfloat16)


def solution(mesh):
    in_specs = (
        P(("blk", "uly"), None),
        P(),
        P(),
        P(),
        P(None, "uly", None),
        P("uly", None),
        P(),
        P(),
    )
    out_specs = P(("blk", "uly"), None)
    return jax.shard_map(
        on_device, mesh=mesh, in_specs=in_specs, out_specs=out_specs, check_vma=False
    )
```

profile of v0, /device:TPU:4, one launch (start us, length us, event | category | flops | bytes accessed | tf_op | source)
XLA Modules:
  0.0 685.6 jit_solution(6186179026058369950)
XLA Ops:
  9.7 1.9 fusion.386
  11.7 31.2 %all-gather.2.cloned.1.call-done = bf16[384,3072]{1,0:T(8,128)(2,1)} async-done(((bf16[48,3072]{1,0:T(8,128)(2,1)}), bf16[384,3072]{1,0:T(8,128)(2,1)}) %all-gather.2.cloned.1.call-update) | async-done | bytes 2359312 | tf_op jit(solution)/shard_map/all_gather | solution.py:29
  42.9 6.9 %fusion.378 = bf16[384,3,384]{2,0,1:T(8,128)(2,1)S(1)} fusion(bf16[3072,3,384]{2,0,1:T(8,128)(2,1)} %param.62, bf16[384,3072]{1,0:T(8,128)(2,1)} %all-gather.2.cloned.1.call-done), kind=kOutput, calls=%fused_computation.479 | convolution fusion | flops 2718351360 | bytes 10321920 | tf_op jit(solution)/shard_map/td,dhe->the/dot_general | solution.py:27
  51.6 7.6 %collective-permute-start = (bf16[384,3,256]{2,0,1:T(8,128)(2,1)}, bf16[384,3,256]{2,0,1:T(8,128)(2,1)}, u32[]{:S(2)}, u32[]{:S(2)}) collective-permute-start(bf16[384,3,256]{2,0,1:T(8,128)(2,1)} %slice.214), channel_id=1, source_target_pairs={{96,0},{104,8},{112,16},{120,24},{128,32},{136,40},{144,48},{152,5... | collective-permute-start | bytes 1769480 | tf_op jit(solution)/shard_map/ppermute | solution.py:14
  59.2 1.9 collective-permute-start.1
  61.2 1.9 collective-permute-start.2
  63.1 1.9 collective-permute-start.3
  65.0 1.9 collective-permute-start.4
  67.0 18.3 %collective-permute-done = bf16[384,3,256]{2,0,1:T(8,128)(2,1)} collective-permute-done((bf16[384,3,256]{2,0,1:T(8,128)(2,1)}, bf16[384,3,256]{2,0,1:T(8,128)(2,1)}, u32[]{:S(2)}, u32[]{:S(2)}) %collective-permute-start) | collective-permute-done | bytes 589856 | tf_op jit(solution)/shard_map/ppermute | solution.py:14
  85.3 6.3 collective-permute-start.5
  91.6 34.4 %collective-permute-done.1 = bf16[384,3,256]{2,0,1:T(8,128)(2,1)} collective-permute-done((bf16[384,3,256]{2,0,1:T(8,128)(2,1)}, bf16[384,3,256]{2,0,1:T(8,128)(2,1)}, u32[]{:S(2)}, u32[]{:S(2)}) %collective-permute-start.1) | collective-permute-done | bytes 589856 | tf_op jit(solution)/shard_map/ppermute | solution.py:14
  126.0 1.9 collective-permute-start.6
  127.9 23.2 %collective-permute-done.2 = bf16[384,3,256]{2,0,1:T(8,128)(2,1)} collective-permute-done((bf16[384,3,256]{2,0,1:T(8,128)(2,1)}, bf16[384,3,256]{2,0,1:T(8,128)(2,1)}, u32[]{:S(2)}, u32[]{:S(2)}) %collective-permute-start.2) | collective-permute-done | bytes 589856 | tf_op jit(solution)/shard_map/ppermute | solution.py:14
  151.1 1.9 collective-permute-start.7
  153.0 12.4 %collective-permute-done.3 = bf16[384,3,256]{2,0,1:T(8,128)(2,1)} collective-permute-done((bf16[384,3,256]{2,0,1:T(8,128)(2,1)}, bf16[384,3,256]{2,0,1:T(8,128)(2,1)}, u32[]{:S(2)}, u32[]{:S(2)}) %collective-permute-start.3) | collective-permute-done | bytes 589856 | tf_op jit(solution)/shard_map/ppermute | solution.py:14
  165.4 7.0 %collective-permute-start.8 = (bf16[384,3,256]{2,0,1:T(8,128)(2,1)}, bf16[384,3,256]{2,0,1:T(8,128)(2,1)}, u32[]{:S(2)}, u32[]{:S(2)}) collective-permute-start(bf16[384,3,256]{2,0,1:T(8,128)(2,1)} %slice.214), channel_id=1, source_target_pairs={{32,0},{40,8},{48,16},{56,24},{64,32},{72,40},{80,48},{88,56},{96,... | collective-permute-start | bytes 1769480 | tf_op jit(solution)/shard_map/ppermute | solution.py:14
  172.4 17.0 %collective-permute-start.9 = (bf16[384,3,256]{2,0,1:T(8,128)(2,1)}, bf16[384,3,256]{2,0,1:T(8,128)(2,1)}, u32[]{:S(2)}, u32[]{:S(2)}) collective-permute-start(bf16[384,3,256]{2,0,1:T(8,128)(2,1)} %slice.214), channel_id=1, source_target_pairs={{24,0},{32,8},{40,16},{48,24},{56,32},{64,40},{72,48},{80,56},{88,... | collective-permute-start | bytes 1769480 | tf_op jit(solution)/shard_map/ppermute | solution.py:14
  189.4 1.9 collective-permute-start.10
  191.4 2.5 collective-permute-start.11
  193.9 23.3 %collective-permute-done.7 = bf16[384,3,256]{2,0,1:T(8,128)(2,1)} collective-permute-done((bf16[384,3,256]{2,0,1:T(8,128)(2,1)}, bf16[384,3,256]{2,0,1:T(8,128)(2,1)}, u32[]{:S(2)}, u32[]{:S(2)}) %collective-permute-start.7) | collective-permute-done | bytes 589856 | tf_op jit(solution)/shard_map/ppermute | solution.py:14
  217.1 21.0 %collective-permute-start.12 = (bf16[384,3,256]{2,0,1:T(8,128)(2,1)}, bf16[384,3,256]{2,0,1:T(8,128)(2,1)}, u32[]{:S(2)}, u32[]{:S(2)}) collective-permute-start(bf16[384,3,256]{2,0,1:T(8,128)(2,1)} %slice.214), channel_id=1, source_target_pairs={{0,8},{8,16},{16,24},{24,32},{32,40},{40,48},{48,56},{56,64},{64,7... | collective-permute-start | bytes 1769480 | tf_op jit(solution)/shard_map/ppermute | solution.py:14
  238.1 12.1 %collective-permute-start.13 = (bf16[384,3,256]{2,0,1:T(8,128)(2,1)}, bf16[384,3,256]{2,0,1:T(8,128)(2,1)}, u32[]{:S(2)}, u32[]{:S(2)}) collective-permute-start(bf16[384,3,256]{2,0,1:T(8,128)(2,1)} %slice.214), channel_id=1, source_target_pairs={{0,16},{8,24},{16,32},{24,40},{32,48},{40,56},{48,64},{56,72},{64,... | collective-permute-start | bytes 1769480 | tf_op jit(solution)/shard_map/ppermute | solution.py:14
  250.2 21.8 %collective-permute-done.9 = bf16[384,3,256]{2,0,1:T(8,128)(2,1)} collective-permute-done((bf16[384,3,256]{2,0,1:T(8,128)(2,1)}, bf16[384,3,256]{2,0,1:T(8,128)(2,1)}, u32[]{:S(2)}, u32[]{:S(2)}) %collective-permute-start.9) | collective-permute-done | bytes 589856 | tf_op jit(solution)/shard_map/ppermute | solution.py:14
  272.0 27.5 %collective-permute-start.14 = (bf16[384,3,256]{2,0,1:T(8,128)(2,1)}, bf16[384,3,256]{2,0,1:T(8,128)(2,1)}, u32[]{:S(2)}, u32[]{:S(2)}) collective-permute-start(bf16[384,3,256]{2,0,1:T(8,128)(2,1)} %slice.214), channel_id=1, source_target_pairs={{0,24},{8,32},{16,40},{24,48},{32,56},{40,64},{48,72},{56,80},{64,... | collective-permute-start | bytes 1769480 | tf_op jit(solution)/shard_map/ppermute | solution.py:14
  299.5 64.9 %collective-permute-start.15 = (bf16[384,3,256]{2,0,1:T(8,128)(2,1)}, bf16[384,3,256]{2,0,1:T(8,128)(2,1)}, u32[]{:S(2)}, u32[]{:S(2)}) collective-permute-start(bf16[384,3,256]{2,0,1:T(8,128)(2,1)} %slice.214), channel_id=1, source_target_pairs={{0,32},{8,40},{16,48},{24,56},{32,64},{40,72},{48,80},{56,88},{64,... | collective-permute-start | bytes 1769480 | tf_op jit(solution)/shard_map/ppermute | solution.py:14
  364.4 11.6 %collective-permute-start.16 = (bf16[384,3,256]{2,0,1:T(8,128)(2,1)}, bf16[384,3,256]{2,0,1:T(8,128)(2,1)}, u32[]{:S(2)}, u32[]{:S(2)}) collective-permute-start(bf16[384,3,256]{2,0,1:T(8,128)(2,1)} %slice.214), channel_id=1, source_target_pairs={{0,40},{8,48},{16,56},{24,64},{32,72},{40,80},{48,88},{56,96},{64,... | collective-permute-start | bytes 1769480 | tf_op jit(solution)/shard_map/ppermute | solution.py:14
  376.0 1.9 collective-permute-start.17
  378.0 1.9 collective-permute-start.18
  379.9 1.9 collective-permute-start.19
  381.9 7.5 %collective-permute-done.15 = bf16[384,3,256]{2,0,1:T(8,128)(2,1)} collective-permute-done((bf16[384,3,256]{2,0,1:T(8,128)(2,1)}, bf16[384,3,256]{2,0,1:T(8,128)(2,1)}, u32[]{:S(2)}, u32[]{:S(2)}) %collective-permute-start.15) | collective-permute-done | bytes 589856 | tf_op jit(solution)/shard_map/ppermute | solution.py:14
  389.3 1.9 collective-permute-start.20
  391.2 26.1 %collective-permute-done.16 = bf16[384,3,256]{2,0,1:T(8,128)(2,1)} collective-permute-done((bf16[384,3,256]{2,0,1:T(8,128)(2,1)}, bf16[384,3,256]{2,0,1:T(8,128)(2,1)}, u32[]{:S(2)}, u32[]{:S(2)}) %collective-permute-start.16) | collective-permute-done | bytes 589856 | tf_op jit(solution)/shard_map/ppermute | solution.py:14
  417.3 13.9 %collective-permute-start.21 = (bf16[384,3,256]{2,0,1:T(8,128)(2,1)}, bf16[384,3,256]{2,0,1:T(8,128)(2,1)}, u32[]{:S(2)}, u32[]{:S(2)}) collective-permute-start(bf16[384,3,256]{2,0,1:T(8,128)(2,1)} %slice.214), channel_id=1, source_target_pairs={{0,80},{8,88},{16,96},{24,104},{32,112},{40,120},{48,128},{56,136}... | collective-permute-start | bytes 1769480 | tf_op jit(solution)/shard_map/ppermute | solution.py:14
  431.3 12.6 %collective-permute-done.17 = bf16[384,3,256]{2,0,1:T(8,128)(2,1)} collective-permute-done((bf16[384,3,256]{2,0,1:T(8,128)(2,1)}, bf16[384,3,256]{2,0,1:T(8,128)(2,1)}, u32[]{:S(2)}, u32[]{:S(2)}) %collective-permute-start.17) | collective-permute-done | bytes 589856 | tf_op jit(solution)/shard_map/ppermute | solution.py:14
  443.8 1.9 collective-permute-start.22
  445.8 30.3 %collective-permute-done.18 = bf16[384,3,256]{2,0,1:T(8,128)(2,1)} collective-permute-done((bf16[384,3,256]{2,0,1:T(8,128)(2,1)}, bf16[384,3,256]{2,0,1:T(8,128)(2,1)}, u32[]{:S(2)}, u32[]{:S(2)}) %collective-permute-start.18) | collective-permute-done | bytes 589856 | tf_op jit(solution)/shard_map/ppermute | solution.py:14
  476.1 1.9 collective-permute-start.23
  573.9 5.5 conditional.25
  573.9 1.4 fusion
  577.7 1.7 convolution_add_fusion
  579.7 8.1 %conditional.34 = ((f32[3,384]{1,0:T(4,128)}, f32[3,384]{1,0:T(4,128)S(1)}, f32[3,384,128]{2,1,0:T(8,128)S(1)})) conditional(s32[]{:T(128)} %bitcast.106, (f32[3,384]{1,0:T(4,128)}, f32[3,384]{1,0:T(4,128)S(1)}, f32[3,384,128]{2,1,0:T(8,128)S(1)}) %get-tuple-element.1021, (pred[1]{0:T(512)(128)(4,1)}, bf16[384,3,256]{2,0,1:T(8,128)(2,1)}, ...), branch_computations={%region_38.39_spmd, %region_39.42_spmd} | conditional | flops 232540416 | bytes 7447585 | solution.py:80
  587.8 5.6 conditional.35
  591.6 1.8 convolution_add_fusion.10
  593.4 6.3 conditional.37
  598.0 1.8 convolution_add_fusion.12
  599.8 5.6 conditional.39
  599.8 1.4 fusion.211
  603.6 1.8 convolution_add_fusion.14
  605.4 5.6 conditional.40
  605.4 1.4 fusion.226
  609.2 1.8 convolution_add_fusion.15
  611.0 6.0 conditional.41
  615.2 1.8 convolution_add_fusion.16
  617.0 5.6 conditional.43
  617.1 1.4 fusion.271
  620.9 1.8 convolution_add_fusion.18
  622.7 5.6 conditional.44
  622.7 1.4 fusion.286
  626.5 1.8 convolution_add_fusion.19
  628.3 5.6 conditional.45
  632.1 1.8 convolution_add_fusion.20
  634.5 2.8 convolution_convert_fusion
  637.4 39.5 %reduce-scatter.2.cloned.1.call-done = bf16[48,3072]{1,0:T(8,128)(2,1)} async-done(((bf16[384,3072]{1,0:T(8,128)(2,1)}), bf16[48,3072]{1,0:T(8,128)(2,1)}) %reduce-scatter.2.cloned.1.call-update) | async-done | bytes 294928 | tf_op jit(solution)/shard_map/reduce_scatter | solution.py:101
  676.8 1.7 multiply_convert_fusion
  (94 shorter events, 37.3 us)
Async XLA Ops:
  6.5 627.9 %copy-start = (bf16[384,3072]{1,0:T(8,128)(2,1)S(1)}, bf16[384,3072]{1,0:T(8,128)(2,1)}, u32[]{:S(2)}) copy-start(bf16[384,3072]{1,0:T(8,128)(2,1)} %param.63) | copy-start | bytes 7077892
  6.5 36.4 %all-gather.2.cloned.1.call-start = ((), (), s32[]{:S(2)}) async-start(), calls=%async_computation.1 | async-start | bytes 2654208 | tf_op jit(solution)/shard_map/all_gather | solution.py:29
  11.6 466.4 %copy-start.2 = (s32[32]{0:T(128)S(1)}, s32[32]{0:T(128)}, u32[]{:S(2)}) copy-start(s32[32]{0:T(128)} %param.64) | copy-start | bytes 388
  11.6 469.6 %copy-start.4 = (s32[32,2]{0,1:T(2,128)S(1)}, s32[32,2]{0,1:T(2,128)}, u32[]{:S(2)}) copy-start(s32[32,2]{0,1:T(2,128)} %param.65) | copy-start | bytes 772
  11.6 665.2 %reduce-scatter.2.cloned.1.call-start = ((), (), s32[]{:S(2)}) async-start(), calls=%async_computation.2 | async-start | bytes 2654208 | tf_op jit(solution)/shard_map/reduce_scatter | solution.py:101
  49.8 0.9 copy-start.1
  51.6 33.7 %collective-permute-start = (bf16[384,3,256]{2,0,1:T(8,128)(2,1)}, bf16[384,3,256]{2,0,1:T(8,128)(2,1)}, u32[]{:S(2)}, u32[]{:S(2)}) collective-permute-start(bf16[384,3,256]{2,0,1:T(8,128)(2,1)} %slice.214), channel_id=1, source_target_pairs={{96,0},{104,8},{112,16},{120,24},{128,32},{136,40},{144,48},{152,5... | collective-permute-start | bytes 1769480 | tf_op jit(solution)/shard_map/ppermute | solution.py:14
  59.2 66.8 %collective-permute-start.1 = (bf16[384,3,256]{2,0,1:T(8,128)(2,1)}, bf16[384,3,256]{2,0,1:T(8,128)(2,1)}, u32[]{:S(2)}, u32[]{:S(2)}) collective-permute-start(bf16[384,3,256]{2,0,1:T(8,128)(2,1)} %slice.214), channel_id=1, source_target_pairs={{88,0},{96,8},{104,16},{112,24},{120,32},{128,40},{136,48},{144,56... | collective-permute-start | bytes 1769480 | tf_op jit(solution)/shard_map/ppermute | solution.py:14
  61.2 90.0 %collective-permute-start.2 = (bf16[384,3,256]{2,0,1:T(8,128)(2,1)}, bf16[384,3,256]{2,0,1:T(8,128)(2,1)}, u32[]{:S(2)}, u32[]{:S(2)}) collective-permute-start(bf16[384,3,256]{2,0,1:T(8,128)(2,1)} %slice.214), channel_id=1, source_target_pairs={{80,0},{88,8},{96,16},{104,24},{112,32},{120,40},{128,48},{136,56}... | collective-permute-start | bytes 1769480 | tf_op jit(solution)/shard_map/ppermute | solution.py:14
  63.1 102.3 %collective-permute-start.3 = (bf16[384,3,256]{2,0,1:T(8,128)(2,1)}, bf16[384,3,256]{2,0,1:T(8,128)(2,1)}, u32[]{:S(2)}, u32[]{:S(2)}) collective-permute-start(bf16[384,3,256]{2,0,1:T(8,128)(2,1)} %slice.214), channel_id=1, source_target_pairs={{72,0},{80,8},{88,16},{96,24},{104,32},{112,40},{120,48},{128,56},... | collective-permute-start | bytes 1769480 | tf_op jit(solution)/shard_map/ppermute | solution.py:14
  65.0 107.4 %collective-permute-start.4 = (bf16[384,3,256]{2,0,1:T(8,128)(2,1)}, bf16[384,3,256]{2,0,1:T(8,128)(2,1)}, u32[]{:S(2)}, u32[]{:S(2)}) collective-permute-start(bf16[384,3,256]{2,0,1:T(8,128)(2,1)} %slice.214), channel_id=1, source_target_pairs={{64,0},{72,8},{80,16},{88,24},{96,32},{104,40},{112,48},{120,56},{... | collective-permute-start | bytes 1769480 | tf_op jit(solution)/shard_map/ppermute | solution.py:14
  85.3 104.2 %collective-permute-start.5 = (bf16[384,3,256]{2,0,1:T(8,128)(2,1)}, bf16[384,3,256]{2,0,1:T(8,128)(2,1)}, u32[]{:S(2)}, u32[]{:S(2)}) collective-permute-start(bf16[384,3,256]{2,0,1:T(8,128)(2,1)} %slice.214), channel_id=1, source_target_pairs={{56,0},{64,8},{72,16},{80,24},{88,32},{96,40},{104,48},{112,56},{1... | collective-permute-start | bytes 1769480 | tf_op jit(solution)/shard_map/ppermute | solution.py:14
  126.0 65.4 %collective-permute-start.6 = (bf16[384,3,256]{2,0,1:T(8,128)(2,1)}, bf16[384,3,256]{2,0,1:T(8,128)(2,1)}, u32[]{:S(2)}, u32[]{:S(2)}) collective-permute-start(bf16[384,3,256]{2,0,1:T(8,128)(2,1)} %slice.214), channel_id=1, source_target_pairs={{48,0},{56,8},{64,16},{72,24},{80,32},{88,40},{96,48},{104,56},{11... | collective-permute-start | bytes 1769480 | tf_op jit(solution)/shard_map/ppermute | solution.py:14
  151.1 66.0 %collective-permute-start.7 = (bf16[384,3,256]{2,0,1:T(8,128)(2,1)}, bf16[384,3,256]{2,0,1:T(8,128)(2,1)}, u32[]{:S(2)}, u32[]{:S(2)}) collective-permute-start(bf16[384,3,256]{2,0,1:T(8,128)(2,1)} %slice.214), channel_id=1, source_target_pairs={{40,0},{48,8},{56,16},{64,24},{72,32},{80,40},{88,48},{96,56},{104... | collective-permute-start | bytes 1769480 | tf_op jit(solution)/shard_map/ppermute | solution.py:14
  165.4 72.7 %collective-permute-start.8 = (bf16[384,3,256]{2,0,1:T(8,128)(2,1)}, bf16[384,3,256]{2,0,1:T(8,128)(2,1)}, u32[]{:S(2)}, u32[]{:S(2)}) collective-permute-start(bf16[384,3,256]{2,0,1:T(8,128)(2,1)} %slice.214), channel_id=1, source_target_pairs={{32,0},{40,8},{48,16},{56,24},{64,32},{72,40},{80,48},{88,56},{96,... | collective-permute-start | bytes 1769480 | tf_op jit(solution)/shard_map/ppermute | solution.py:14
  172.4 99.6 %collective-permute-start.9 = (bf16[384,3,256]{2,0,1:T(8,128)(2,1)}, bf16[384,3,256]{2,0,1:T(8,128)(2,1)}, u32[]{:S(2)}, u32[]{:S(2)}) collective-permute-start(bf16[384,3,256]{2,0,1:T(8,128)(2,1)} %slice.214), channel_id=1, source_target_pairs={{24,0},{32,8},{40,16},{48,24},{56,32},{64,40},{72,48},{80,56},{88,... | collective-permute-start | bytes 1769480 | tf_op jit(solution)/shard_map/ppermute | solution.py:14
  189.4 110.1 %collective-permute-start.10 = (bf16[384,3,256]{2,0,1:T(8,128)(2,1)}, bf16[384,3,256]{2,0,1:T(8,128)(2,1)}, u32[]{:S(2)}, u32[]{:S(2)}) collective-permute-start(bf16[384,3,256]{2,0,1:T(8,128)(2,1)} %slice.214), channel_id=1, source_target_pairs={{16,0},{24,8},{32,16},{40,24},{48,32},{56,40},{64,48},{72,56},{80,... | collective-permute-start | bytes 1769480 | tf_op jit(solution)/shard_map/ppermute | solution.py:14
  191.4 173.0 %collective-permute-start.11 = (bf16[384,3,256]{2,0,1:T(8,128)(2,1)}, bf16[384,3,256]{2,0,1:T(8,128)(2,1)}, u32[]{:S(2)}, u32[]{:S(2)}) collective-permute-start(bf16[384,3,256]{2,0,1:T(8,128)(2,1)} %slice.214), channel_id=1, source_target_pairs={{8,0},{16,8},{24,16},{32,24},{40,32},{48,40},{56,48},{64,56},{72,6... | collective-permute-start | bytes 1769480 | tf_op jit(solution)/shard_map/ppermute | solution.py:14
  217.1 158.9 %collective-permute-start.12 = (bf16[384,3,256]{2,0,1:T(8,128)(2,1)}, bf16[384,3,256]{2,0,1:T(8,128)(2,1)}, u32[]{:S(2)}, u32[]{:S(2)}) collective-permute-start(bf16[384,3,256]{2,0,1:T(8,128)(2,1)} %slice.214), channel_id=1, source_target_pairs={{0,8},{8,16},{16,24},{24,32},{32,40},{40,48},{48,56},{56,64},{64,7... | collective-permute-start | bytes 1769480 | tf_op jit(solution)/shard_map/ppermute | solution.py:14
  238.1 139.8 %collective-permute-start.13 = (bf16[384,3,256]{2,0,1:T(8,128)(2,1)}, bf16[384,3,256]{2,0,1:T(8,128)(2,1)}, u32[]{:S(2)}, u32[]{:S(2)}) collective-permute-start(bf16[384,3,256]{2,0,1:T(8,128)(2,1)} %slice.214), channel_id=1, source_target_pairs={{0,16},{8,24},{16,32},{24,40},{32,48},{40,56},{48,64},{56,72},{64,... | collective-permute-start | bytes 1769480 | tf_op jit(solution)/shard_map/ppermute | solution.py:14
  272.0 107.9 %collective-permute-start.14 = (bf16[384,3,256]{2,0,1:T(8,128)(2,1)}, bf16[384,3,256]{2,0,1:T(8,128)(2,1)}, u32[]{:S(2)}, u32[]{:S(2)}) collective-permute-start(bf16[384,3,256]{2,0,1:T(8,128)(2,1)} %slice.214), channel_id=1, source_target_pairs={{0,24},{8,32},{16,40},{24,48},{32,56},{40,64},{48,72},{56,80},{64,... | collective-permute-start | bytes 1769480 | tf_op jit(solution)/shard_map/ppermute | solution.py:14
  299.5 89.8 %collective-permute-start.15 = (bf16[384,3,256]{2,0,1:T(8,128)(2,1)}, bf16[384,3,256]{2,0,1:T(8,128)(2,1)}, u32[]{:S(2)}, u32[]{:S(2)}) collective-permute-start(bf16[384,3,256]{2,0,1:T(8,128)(2,1)} %slice.214), channel_id=1, source_target_pairs={{0,32},{8,40},{16,48},{24,56},{32,64},{40,72},{48,80},{56,88},{64,... | collective-permute-start | bytes 1769480 | tf_op jit(solution)/shard_map/ppermute | solution.py:14
  364.4 52.9 %collective-permute-start.16 = (bf16[384,3,256]{2,0,1:T(8,128)(2,1)}, bf16[384,3,256]{2,0,1:T(8,128)(2,1)}, u32[]{:S(2)}, u32[]{:S(2)}) collective-permute-start(bf16[384,3,256]{2,0,1:T(8,128)(2,1)} %slice.214), channel_id=1, source_target_pairs={{0,40},{8,48},{16,56},{24,64},{32,72},{40,80},{48,88},{56,96},{64,... | collective-permute-start | bytes 1769480 | tf_op jit(solution)/shard_map/ppermute | solution.py:14
  376.0 67.8 %collective-permute-start.17 = (bf16[384,3,256]{2,0,1:T(8,128)(2,1)}, bf16[384,3,256]{2,0,1:T(8,128)(2,1)}, u32[]{:S(2)}, u32[]{:S(2)}) collective-permute-start(bf16[384,3,256]{2,0,1:T(8,128)(2,1)} %slice.214), channel_id=1, source_target_pairs={{0,48},{8,56},{16,64},{24,72},{32,80},{40,88},{48,96},{56,104},{64... | collective-permute-start | bytes 1769480 | tf_op jit(solution)/shard_map/ppermute | solution.py:14
  378.0 98.1 %collective-permute-start.18 = (bf16[384,3,256]{2,0,1:T(8,128)(2,1)}, bf16[384,3,256]{2,0,1:T(8,128)(2,1)}, u32[]{:S(2)}, u32[]{:S(2)}) collective-permute-start(bf16[384,3,256]{2,0,1:T(8,128)(2,1)} %slice.214), channel_id=1, source_target_pairs={{0,56},{8,64},{16,72},{24,80},{32,88},{40,96},{48,104},{56,112},{6... | collective-permute-start | bytes 1769480 | tf_op jit(solution)/shard_map/ppermute | solution.py:14
  379.9 248.4 %collective-permute-start.19 = (bf16[384,3,256]{2,0,1:T(8,128)(2,1)}, bf16[384,3,256]{2,0,1:T(8,128)(2,1)}, u32[]{:S(2)}, u32[]{:S(2)}) collective-permute-start(bf16[384,3,256]{2,0,1:T(8,128)(2,1)} %slice.214), channel_id=1, source_target_pairs={{0,64},{8,72},{16,80},{24,88},{32,96},{40,104},{48,112},{56,120},{... | collective-permute-start | bytes 1769480 | tf_op jit(solution)/shard_map/ppermute | solution.py:14
  389.3 244.6 %collective-permute-start.20 = (bf16[384,3,256]{2,0,1:T(8,128)(2,1)}, bf16[384,3,256]{2,0,1:T(8,128)(2,1)}, u32[]{:S(2)}, u32[]{:S(2)}) collective-permute-start(bf16[384,3,256]{2,0,1:T(8,128)(2,1)} %slice.214), channel_id=1, source_target_pairs={{0,72},{8,80},{16,88},{24,96},{32,104},{40,112},{48,120},{56,128},... | collective-permute-start | bytes 1769480 | tf_op jit(solution)/shard_map/ppermute | solution.py:14
  417.3 216.6 %collective-permute-start.21 = (bf16[384,3,256]{2,0,1:T(8,128)(2,1)}, bf16[384,3,256]{2,0,1:T(8,128)(2,1)}, u32[]{:S(2)}, u32[]{:S(2)}) collective-permute-start(bf16[384,3,256]{2,0,1:T(8,128)(2,1)} %slice.214), channel_id=1, source_target_pairs={{0,80},{8,88},{16,96},{24,104},{32,112},{40,120},{48,128},{56,136}... | collective-permute-start | bytes 1769480 | tf_op jit(solution)/shard_map/ppermute | solution.py:14
  443.8 190.1 %collective-permute-start.22 = (bf16[384,3,256]{2,0,1:T(8,128)(2,1)}, bf16[384,3,256]{2,0,1:T(8,128)(2,1)}, u32[]{:S(2)}, u32[]{:S(2)}) collective-permute-start(bf16[384,3,256]{2,0,1:T(8,128)(2,1)} %slice.214), channel_id=1, source_target_pairs={{0,88},{8,96},{16,104},{24,112},{32,120},{40,128},{48,136},{56,144... | collective-permute-start | bytes 1769480 | tf_op jit(solution)/shard_map/ppermute | solution.py:14
  476.1 158.1 %collective-permute-start.23 = (bf16[384,3,256]{2,0,1:T(8,128)(2,1)}, bf16[384,3,256]{2,0,1:T(8,128)(2,1)}, u32[]{:S(2)}, u32[]{:S(2)}) collective-permute-start(bf16[384,3,256]{2,0,1:T(8,128)(2,1)} %slice.214), channel_id=1, source_target_pairs={{0,96},{8,104},{16,112},{24,120},{32,128},{40,136},{48,144},{56,15... | collective-permute-start | bytes 1769480 | tf_op jit(solution)/shard_map/ppermute | solution.py:14
  637.3 39.5 %copy-start.3 = (f32[3072]{0:T(1024)S(1)}, f32[3072]{0:T(1024)}, u32[]{:S(2)}) copy-start(f32[3072]{0:T(1024)} %param.61) | copy-start | bytes 36868
Sparse Core Ops, SparseCore 0:
  11.7 31.0 all-gather.1
  637.5 39.3 reduce-scatter.1
where the time goes:
time: 697 us; the launch traced here: 686 us
  waiting for transfers between devices  281 us (40%)
  starting transfers between devices  216 us (31%)
  between operations  107 us (15%)
  matrix products  38.1 us (5%)
  other arithmetic  25.2 us (4%)
  local copies, waits for them, and re-layouts  9.26 us (1%)
  loops' own time  9.18 us (1%)
    ppermute x24, starting transfers between devices, from_behind(): return lax.ppermute(block, axis, route)  216 us
    ppermute x24, waiting for transfers between devices, from_behind(): return lax.ppermute(block, axis, route)  210 us
    reduce_scatter x1, waiting for transfers between devices, on_device(): lax.psum_scatter(jnp.dot(attn, w_out, preferred_element_type=jnp.float32)...  39.5 us
    all_gather x1, waiting for transfers between devices, on_device(): lax.all_gather(normed, 'uly', axis=0, tiled=True)  31.2 us
    dot_general x9, matrix products, compute(): jnp.einsum('hqk,khd->hqd', weights, kv_tile[:, :, head_dim:], preferred_e...  15.8 us
  transfers between devices with their start and end apart: 26, of which 12 were waited for; matrix products, arithmetic and copies ran while one was open for 8% of the time, Pallas kernels for 0%

commit v1 on v0

--- a/solution.py
+++ b/solution.py
@@ -26,7 +26,9 @@
     head_dim = w_qkv.shape[2] // 3
     qkv = jnp.einsum(
         "td,dhe->the",
-        lax.all_gather(normed, "uly", axis=0, tiled=True),
+        jnp.concatenate(
+            lax.all_to_all(jnp.stack([normed] * lax.axis_size("uly")), "uly", 0, 0), axis=0
+        ),
         w_qkv,
         preferred_element_type=jnp.float32,
     ).astype(jnp.bfloat16)

time: 697 us -> 670 us (0.961)
  starting transfers between devices: 216 us -> 168 us
  blocking collectives: 0 us -> 34.9 us
  waiting for transfers between devices: 281 us -> 273 us
    ppermute x24, starting transfers between devices: 216 us -> 168 us  [from_behind(): return lax.ppermute(block, axis, route)]
    all_to_all x0 -> x1, blocking collectives: none -> 34.9 us  [on_device(): lax.all_to_all(jnp.stack([normed] * lax.axis_size('uly')), 'uly', 0, 0)]
    all_gather x1 -> x0, waiting for transfers between devices: 31.2 us -> none  [on_device(): lax.all_gather(normed, 'uly', axis=0, tiled=True)]
    reduce_scatter x1, waiting for transfers between devices: 39.5 us -> 59.5 us  [on_device(): lax.psum_scatter(jnp.dot(attn, w_out, preferred_element_type=jnp.float32)...]
  transfers between devices with their start and end apart: 26 -> 25, of which waited for: 12 -> 11; matrix products, arithmetic and copies ran while one was open for 8% -> 8% of each run, Pallas kernels for 0% -> 0%
where the time goes in v1:
time: 670 us; the launch traced here: 659 us
  waiting for transfers between devices  273 us (41%)
  starting transfers between devices  168 us (25%)
  between operations  106 us (16%)
  blocking collectives  34.9 us (5%)
  matrix products  34.4 us (5%)
  other arithmetic  24.5 us (4%)
  local copies, waits for them, and re-layouts  9.49 us (1%)
  loops' own time  9.06 us (1%)
    ppermute x24, waiting for transfers between devices, from_behind(): return lax.ppermute(block, axis, route)  213 us
    ppermute x24, starting transfers between devices, from_behind(): return lax.ppermute(block, axis, route)  168 us
    reduce_scatter x1, waiting for transfers between devices, on_device(): lax.psum_scatter(jnp.dot(attn, w_out, preferred_element_type=jnp.float32)...  59.5 us
    all_to_all x1, blocking collectives, on_device(): lax.all_to_all(jnp.stack([normed] * lax.axis_size('uly')), 'uly', 0, 0)  34.9 us
    dot_general x9, matrix products, compute(): jnp.einsum('hqk,khd->hqd', weights, kv_tile[:, :, head_dim:], preferred_e...  15.8 us
  transfers between devices with their start and end apart: 25, of which 11 were waited for; matrix products, arithmetic and copies ran while one was open for 8% of the time, Pallas kernels for 0%

profile of v1, /device:TPU:4, one launch (start us, length us, event | category | flops | bytes accessed | tf_op | source)
XLA Modules:
  0.0 659.0 jit_solution(14448534223743909291)
XLA Ops:
  11.2 34.9 %all_to_all.5 = bf16[8,48,3072]{2,1,0:T(8,128)(2,1)S(1)} all-to-all(bf16[8,48,3072]{2,1,0:T(8,128)(2,1)S(1)} %stack.2), channel_id=1, replica_groups=mesh['blk'=32,'uly'=8] {'uly'}, dimensions={0} | all-to-all | bytes 4718592 | tf_op jit(solution)/shard_map/all_to_all | solution.py:30
  46.1 3.2 convolution_convert_fusion.1
  51.1 9.0 %collective-permute-start = (bf16[384,3,256]{2,0,1:T(8,128)(2,1)}, bf16[384,3,256]{2,0,1:T(8,128)(2,1)}, u32[]{:S(2)}, u32[]{:S(2)}) collective-permute-start(bf16[384,3,256]{2,0,1:T(8,128)(2,1)} %slice.214), channel_id=1, source_target_pairs={{96,0},{104,8},{112,16},{120,24},{128,32},{136,40},{144,48},{152,5... | collective-permute-start | bytes 1769480 | tf_op jit(solution)/shard_map/ppermute | solution.py:14
  60.2 1.9 collective-permute-start.1
  62.1 1.9 collective-permute-start.2
  64.0 1.9 collective-permute-start.3
  65.9 1.9 collective-permute-start.4
  67.9 17.7 %collective-permute-done = bf16[384,3,256]{2,0,1:T(8,128)(2,1)} collective-permute-done((bf16[384,3,256]{2,0,1:T(8,128)(2,1)}, bf16[384,3,256]{2,0,1:T(8,128)(2,1)}, u32[]{:S(2)}, u32[]{:S(2)}) %collective-permute-start) | collective-permute-done | bytes 589856 | tf_op jit(solution)/shard_map/ppermute | solution.py:14
  85.6 7.6 %collective-permute-start.5 = (bf16[384,3,256]{2,0,1:T(8,128)(2,1)}, bf16[384,3,256]{2,0,1:T(8,128)(2,1)}, u32[]{:S(2)}, u32[]{:S(2)}) collective-permute-start(bf16[384,3,256]{2,0,1:T(8,128)(2,1)} %slice.214), channel_id=1, source_target_pairs={{56,0},{64,8},{72,16},{80,24},{88,32},{96,40},{104,48},{112,56},{1... | collective-permute-start | bytes 1769480 | tf_op jit(solution)/shard_map/ppermute | solution.py:14
  93.2 33.0 %collective-permute-done.1 = bf16[384,3,256]{2,0,1:T(8,128)(2,1)} collective-permute-done((bf16[384,3,256]{2,0,1:T(8,128)(2,1)}, bf16[384,3,256]{2,0,1:T(8,128)(2,1)}, u32[]{:S(2)}, u32[]{:S(2)}) %collective-permute-start.1) | collective-permute-done | bytes 589856 | tf_op jit(solution)/shard_map/ppermute | solution.py:14
  126.1 1.9 collective-permute-start.6
  128.1 21.5 %collective-permute-done.2 = bf16[384,3,256]{2,0,1:T(8,128)(2,1)} collective-permute-done((bf16[384,3,256]{2,0,1:T(8,128)(2,1)}, bf16[384,3,256]{2,0,1:T(8,128)(2,1)}, u32[]{:S(2)}, u32[]{:S(2)}) %collective-permute-start.2) | collective-permute-done | bytes 589856 | tf_op jit(solution)/shard_map/ppermute | solution.py:14
  149.6 1.9 collective-permute-start.7
  151.5 13.0 %collective-permute-done.3 = bf16[384,3,256]{2,0,1:T(8,128)(2,1)} collective-permute-done((bf16[384,3,256]{2,0,1:T(8,128)(2,1)}, bf16[384,3,256]{2,0,1:T(8,128)(2,1)}, u32[]{:S(2)}, u32[]{:S(2)}) %collective-permute-start.3) | collective-permute-done | bytes 589856 | tf_op jit(solution)/shard_map/ppermute | solution.py:14
  164.5 5.3 collective-permute-start.8
  169.8 44.7 %collective-permute-start.9 = (bf16[384,3,256]{2,0,1:T(8,128)(2,1)}, bf16[384,3,256]{2,0,1:T(8,128)(2,1)}, u32[]{:S(2)}, u32[]{:S(2)}) collective-permute-start(bf16[384,3,256]{2,0,1:T(8,128)(2,1)} %slice.214), channel_id=1, source_target_pairs={{24,0},{32,8},{40,16},{48,24},{56,32},{64,40},{72,48},{80,56},{88,... | collective-permute-start | bytes 1769480 | tf_op jit(solution)/shard_map/ppermute | solution.py:14
  214.5 1.9 collective-permute-start.10
  216.5 2.5 collective-permute-start.11
  219.0 8.9 %collective-permute-start.12 = (bf16[384,3,256]{2,0,1:T(8,128)(2,1)}, bf16[384,3,256]{2,0,1:T(8,128)(2,1)}, u32[]{:S(2)}, u32[]{:S(2)}) collective-permute-start(bf16[384,3,256]{2,0,1:T(8,128)(2,1)} %slice.214), channel_id=1, source_target_pairs={{0,8},{8,16},{16,24},{24,32},{32,40},{40,48},{48,56},{56,64},{64,7... | collective-permute-start | bytes 1769480 | tf_op jit(solution)/shard_map/ppermute | solution.py:14
  227.9 5.8 collective-permute-done.8
  233.6 9.2 %collective-permute-start.13 = (bf16[384,3,256]{2,0,1:T(8,128)(2,1)}, bf16[384,3,256]{2,0,1:T(8,128)(2,1)}, u32[]{:S(2)}, u32[]{:S(2)}) collective-permute-start(bf16[384,3,256]{2,0,1:T(8,128)(2,1)} %slice.214), channel_id=1, source_target_pairs={{0,16},{8,24},{16,32},{24,40},{32,48},{40,56},{48,64},{56,72},{64,... | collective-permute-start | bytes 1769480 | tf_op jit(solution)/shard_map/ppermute | solution.py:14
  242.8 13.9 %collective-permute-done.9 = bf16[384,3,256]{2,0,1:T(8,128)(2,1)} collective-permute-done((bf16[384,3,256]{2,0,1:T(8,128)(2,1)}, bf16[384,3,256]{2,0,1:T(8,128)(2,1)}, u32[]{:S(2)}, u32[]{:S(2)}) %collective-permute-start.9) | collective-permute-done | bytes 589856 | tf_op jit(solution)/shard_map/ppermute | solution.py:14
  256.8 8.5 %collective-permute-start.14 = (bf16[384,3,256]{2,0,1:T(8,128)(2,1)}, bf16[384,3,256]{2,0,1:T(8,128)(2,1)}, u32[]{:S(2)}, u32[]{:S(2)}) collective-permute-start(bf16[384,3,256]{2,0,1:T(8,128)(2,1)} %slice.214), channel_id=1, source_target_pairs={{0,24},{8,32},{16,40},{24,48},{32,56},{40,64},{48,72},{56,80},{64,... | collective-permute-start | bytes 1769480 | tf_op jit(solution)/shard_map/ppermute | solution.py:14
  265.3 19.2 %collective-permute-done.10 = bf16[384,3,256]{2,0,1:T(8,128)(2,1)} collective-permute-done((bf16[384,3,256]{2,0,1:T(8,128)(2,1)}, bf16[384,3,256]{2,0,1:T(8,128)(2,1)}, u32[]{:S(2)}, u32[]{:S(2)}) %collective-permute-start.10) | collective-permute-done | bytes 589856 | tf_op jit(solution)/shard_map/ppermute | solution.py:14
  284.5 4.6 collective-permute-start.15
  289.1 39.6 %collective-permute-done.11 = bf16[384,3,256]{2,0,1:T(8,128)(2,1)} collective-permute-done((bf16[384,3,256]{2,0,1:T(8,128)(2,1)}, bf16[384,3,256]{2,0,1:T(8,128)(2,1)}, u32[]{:S(2)}, u32[]{:S(2)}) %collective-permute-start.11) | collective-permute-done | bytes 589856 | tf_op jit(solution)/shard_map/ppermute | solution.py:14
  328.6 1.9 collective-permute-start.16
  330.6 30.7 %collective-permute-start.17 = (bf16[384,3,256]{2,0,1:T(8,128)(2,1)}, bf16[384,3,256]{2,0,1:T(8,128)(2,1)}, u32[]{:S(2)}, u32[]{:S(2)}) collective-permute-start(bf16[384,3,256]{2,0,1:T(8,128)(2,1)} %slice.214), channel_id=1, source_target_pairs={{0,48},{8,56},{16,64},{24,72},{32,80},{40,88},{48,96},{56,104},{64... | collective-permute-start | bytes 1769480 | tf_op jit(solution)/shard_map/ppermute | solution.py:14
  361.3 11.6 %collective-permute-start.18 = (bf16[384,3,256]{2,0,1:T(8,128)(2,1)}, bf16[384,3,256]{2,0,1:T(8,128)(2,1)}, u32[]{:S(2)}, u32[]{:S(2)}) collective-permute-start(bf16[384,3,256]{2,0,1:T(8,128)(2,1)} %slice.214), channel_id=1, source_target_pairs={{0,56},{8,64},{16,72},{24,80},{32,88},{40,96},{48,104},{56,112},{6... | collective-permute-start | bytes 1769480 | tf_op jit(solution)/shard_map/ppermute | solution.py:14
  373.0 1.9 collective-permute-start.19
  374.9 1.9 collective-permute-start.20
  376.9 1.9 collective-permute-start.21
  378.8 18.6 %collective-permute-done.17 = bf16[384,3,256]{2,0,1:T(8,128)(2,1)} collective-permute-done((bf16[384,3,256]{2,0,1:T(8,128)(2,1)}, bf16[384,3,256]{2,0,1:T(8,128)(2,1)}, u32[]{:S(2)}, u32[]{:S(2)}) %collective-permute-start.17) | collective-permute-done | bytes 589856 | tf_op jit(solution)/shard_map/ppermute | solution.py:14
  397.4 1.9 collective-permute-start.22
  399.4 31.0 %collective-permute-done.18 = bf16[384,3,256]{2,0,1:T(8,128)(2,1)} collective-permute-done((bf16[384,3,256]{2,0,1:T(8,128)(2,1)}, bf16[384,3,256]{2,0,1:T(8,128)(2,1)}, u32[]{:S(2)}, u32[]{:S(2)}) %collective-permute-start.18) | collective-permute-done | bytes 589856 | tf_op jit(solution)/shard_map/ppermute | solution.py:14
  430.4 1.9 collective-permute-start.23
  527.5 5.5 conditional.25
  527.5 1.4 fusion
  529.5 1.6 convolution_add_fusion
  533.3 8.1 %conditional.34 = ((f32[3,384]{1,0:T(4,128)}, f32[3,384]{1,0:T(4,128)S(1)}, f32[3,384,128]{2,1,0:T(8,128)S(1)})) conditional(s32[]{:T(128)} %bitcast.106, (f32[3,384]{1,0:T(4,128)}, f32[3,384]{1,0:T(4,128)S(1)}, f32[3,384,128]{2,1,0:T(8,128)S(1)}) %get-tuple-element.1021, (pred[1]{0:T(512)(128)(4,1)}, bf16[384,3,256]{2,0,1:T(8,128)(2,1)}, ...), branch_computations={%region_38.39_spmd, %region_39.42_spmd} | conditional | flops 232540416 | bytes 7447585 | solution.py:82
  541.4 5.6 conditional.35
  541.4 1.4 fusion.151
  544.6 1.8 convolution_add_fusion.10
  547.0 6.3 conditional.37
  547.0 1.4 fusion.181
  551.5 1.8 convolution_add_fusion.12
  553.3 5.6 conditional.39
  553.3 1.4 fusion.211
  556.6 1.8 convolution_add_fusion.14
  558.9 5.6 conditional.40
  562.2 1.8 convolution_add_fusion.15
  564.5 6.0 conditional.41
  564.9 1.4 fusion.241
  568.1 1.8 convolution_add_fusion.16
  570.5 5.6 conditional.43
  573.7 1.8 convolution_add_fusion.18
  576.1 5.6 conditional.44
  579.3 1.8 convolution_add_fusion.19
  581.7 5.6 conditional.45
  581.7 1.4 fusion.301
  584.9 1.8 convolution_add_fusion.20
  587.8 2.8 convolution_convert_fusion
  590.7 59.5 %reduce-scatter.2.cloned.1.call-done = bf16[48,3072]{1,0:T(8,128)(2,1)} async-done(((bf16[384,3072]{1,0:T(8,128)(2,1)}), bf16[48,3072]{1,0:T(8,128)(2,1)}) %reduce-scatter.2.cloned.1.call-update) | async-done | bytes 294928 | tf_op jit(solution)/shard_map/reduce_scatter | solution.py:103
  650.2 1.7 multiply_convert_fusion
  (95 shorter events, 37.1 us)
Async XLA Ops:
  6.5 581.3 %copy-start = (bf16[384,3072]{1,0:T(8,128)(2,1)S(1)}, bf16[384,3072]{1,0:T(8,128)(2,1)}, u32[]{:S(2)}) copy-start(bf16[384,3072]{1,0:T(8,128)(2,1)} %param.63) | copy-start | bytes 7077892
  6.5 643.7 %reduce-scatter.2.cloned.1.call-start = ((), (), s32[]{:S(2)}) async-start(), calls=%async_computation.2 | async-start | bytes 2654208 | tf_op jit(solution)/shard_map/reduce_scatter | solution.py:103
  10.9 35.2 %copy-start.5 = (bf16[3072,3,384]{2,0,1:T(8,128)(2,1)S(1)}, bf16[3072,3,384]{2,0,1:T(8,128)(2,1)}, u32[]{:S(2)}) copy-start(bf16[3072,3,384]{2,0,1:T(8,128)(2,1)} %param.62) | copy-start | bytes 21233668
  46.1 386.3 %copy-start.2 = (s32[32]{0:T(128)S(1)}, s32[32]{0:T(128)}, u32[]{:S(2)}) copy-start(s32[32]{0:T(128)} %param.64) | copy-start | bytes 388
  46.1 389.7 %copy-start.4 = (s32[32,2]{0,1:T(2,128)S(1)}, s32[32,2]{0,1:T(2,128)}, u32[]{:S(2)}) copy-start(s32[32,2]{0,1:T(2,128)} %param.65) | copy-start | bytes 772
  49.3 0.9 copy-start.1
  51.1 34.4 %collective-permute-start = (bf16[384,3,256]{2,0,1:T(8,128)(2,1)}, bf16[384,3,256]{2,0,1:T(8,128)(2,1)}, u32[]{:S(2)}, u32[]{:S(2)}) collective-permute-start(bf16[384,3,256]{2,0,1:T(8,128)(2,1)} %slice.214), channel_id=1, source_target_pairs={{96,0},{104,8},{112,16},{120,24},{128,32},{136,40},{144,48},{152,5... | collective-permute-start | bytes 1769480 | tf_op jit(solution)/shard_map/ppermute | solution.py:14
  60.2 66.0 %collective-permute-start.1 = (bf16[384,3,256]{2,0,1:T(8,128)(2,1)}, bf16[384,3,256]{2,0,1:T(8,128)(2,1)}, u32[]{:S(2)}, u32[]{:S(2)}) collective-permute-start(bf16[384,3,256]{2,0,1:T(8,128)(2,1)} %slice.214), channel_id=1, source_target_pairs={{88,0},{96,8},{104,16},{112,24},{120,32},{128,40},{136,48},{144,56... | collective-permute-start | bytes 1769480 | tf_op jit(solution)/shard_map/ppermute | solution.py:14
  62.1 87.5 %collective-permute-start.2 = (bf16[384,3,256]{2,0,1:T(8,128)(2,1)}, bf16[384,3,256]{2,0,1:T(8,128)(2,1)}, u32[]{:S(2)}, u32[]{:S(2)}) collective-permute-start(bf16[384,3,256]{2,0,1:T(8,128)(2,1)} %slice.214), channel_id=1, source_target_pairs={{80,0},{88,8},{96,16},{104,24},{112,32},{120,40},{128,48},{136,56}... | collective-permute-start | bytes 1769480 | tf_op jit(solution)/shard_map/ppermute | solution.py:14
  64.0 100.5 %collective-permute-start.3 = (bf16[384,3,256]{2,0,1:T(8,128)(2,1)}, bf16[384,3,256]{2,0,1:T(8,128)(2,1)}, u32[]{:S(2)}, u32[]{:S(2)}) collective-permute-start(bf16[384,3,256]{2,0,1:T(8,128)(2,1)} %slice.214), channel_id=1, source_target_pairs={{72,0},{80,8},{88,16},{96,24},{104,32},{112,40},{120,48},{128,56},... | collective-permute-start | bytes 1769480 | tf_op jit(solution)/shard_map/ppermute | solution.py:14
  65.9 103.8 %collective-permute-start.4 = (bf16[384,3,256]{2,0,1:T(8,128)(2,1)}, bf16[384,3,256]{2,0,1:T(8,128)(2,1)}, u32[]{:S(2)}, u32[]{:S(2)}) collective-permute-start(bf16[384,3,256]{2,0,1:T(8,128)(2,1)} %slice.214), channel_id=1, source_target_pairs={{64,0},{72,8},{80,16},{88,24},{96,32},{104,40},{112,48},{120,56},{... | collective-permute-start | bytes 1769480 | tf_op jit(solution)/shard_map/ppermute | solution.py:14
  85.6 129.0 %collective-permute-start.5 = (bf16[384,3,256]{2,0,1:T(8,128)(2,1)}, bf16[384,3,256]{2,0,1:T(8,128)(2,1)}, u32[]{:S(2)}, u32[]{:S(2)}) collective-permute-start(bf16[384,3,256]{2,0,1:T(8,128)(2,1)} %slice.214), channel_id=1, source_target_pairs={{56,0},{64,8},{72,16},{80,24},{88,32},{96,40},{104,48},{112,56},{1... | collective-permute-start | bytes 1769480 | tf_op jit(solution)/shard_map/ppermute | solution.py:14
  126.1 90.3 %collective-permute-start.6 = (bf16[384,3,256]{2,0,1:T(8,128)(2,1)}, bf16[384,3,256]{2,0,1:T(8,128)(2,1)}, u32[]{:S(2)}, u32[]{:S(2)}) collective-permute-start(bf16[384,3,256]{2,0,1:T(8,128)(2,1)} %slice.214), channel_id=1, source_target_pairs={{48,0},{56,8},{64,16},{72,24},{80,32},{88,40},{96,48},{104,56},{11... | collective-permute-start | bytes 1769480 | tf_op jit(solution)/shard_map/ppermute | solution.py:14
  149.6 69.4 %collective-permute-start.7 = (bf16[384,3,256]{2,0,1:T(8,128)(2,1)}, bf16[384,3,256]{2,0,1:T(8,128)(2,1)}, u32[]{:S(2)}, u32[]{:S(2)}) collective-permute-start(bf16[384,3,256]{2,0,1:T(8,128)(2,1)} %slice.214), channel_id=1, source_target_pairs={{40,0},{48,8},{56,16},{64,24},{72,32},{80,40},{88,48},{96,56},{104... | collective-permute-start | bytes 1769480 | tf_op jit(solution)/shard_map/ppermute | solution.py:14
  164.5 69.2 %collective-permute-start.8 = (bf16[384,3,256]{2,0,1:T(8,128)(2,1)}, bf16[384,3,256]{2,0,1:T(8,128)(2,1)}, u32[]{:S(2)}, u32[]{:S(2)}) collective-permute-start(bf16[384,3,256]{2,0,1:T(8,128)(2,1)} %slice.214), channel_id=1, source_target_pairs={{32,0},{40,8},{48,16},{56,24},{64,32},{72,40},{80,48},{88,56},{96,... | collective-permute-start | bytes 1769480 | tf_op jit(solution)/shard_map/ppermute | solution.py:14
  169.8 87.0 %collective-permute-start.9 = (bf16[384,3,256]{2,0,1:T(8,128)(2,1)}, bf16[384,3,256]{2,0,1:T(8,128)(2,1)}, u32[]{:S(2)}, u32[]{:S(2)}) collective-permute-start(bf16[384,3,256]{2,0,1:T(8,128)(2,1)} %slice.214), channel_id=1, source_target_pairs={{24,0},{32,8},{40,16},{48,24},{56,32},{64,40},{72,48},{80,56},{88,... | collective-permute-start | bytes 1769480 | tf_op jit(solution)/shard_map/ppermute | solution.py:14
  214.5 70.0 %collective-permute-start.10 = (bf16[384,3,256]{2,0,1:T(8,128)(2,1)}, bf16[384,3,256]{2,0,1:T(8,128)(2,1)}, u32[]{:S(2)}, u32[]{:S(2)}) collective-permute-start(bf16[384,3,256]{2,0,1:T(8,128)(2,1)} %slice.214), channel_id=1, source_target_pairs={{16,0},{24,8},{32,16},{40,24},{48,32},{56,40},{64,48},{72,56},{80,... | collective-permute-start | bytes 1769480 | tf_op jit(solution)/shard_map/ppermute | solution.py:14
  216.5 112.2 %collective-permute-start.11 = (bf16[384,3,256]{2,0,1:T(8,128)(2,1)}, bf16[384,3,256]{2,0,1:T(8,128)(2,1)}, u32[]{:S(2)}, u32[]{:S(2)}) collective-permute-start(bf16[384,3,256]{2,0,1:T(8,128)(2,1)} %slice.214), channel_id=1, source_target_pairs={{8,0},{16,8},{24,16},{32,24},{40,32},{48,40},{56,48},{64,56},{72,6... | collective-permute-start | bytes 1769480 | tf_op jit(solution)/shard_map/ppermute | solution.py:14
  219.0 111.6 %collective-permute-start.12 = (bf16[384,3,256]{2,0,1:T(8,128)(2,1)}, bf16[384,3,256]{2,0,1:T(8,128)(2,1)}, u32[]{:S(2)}, u32[]{:S(2)}) collective-permute-start(bf16[384,3,256]{2,0,1:T(8,128)(2,1)} %slice.214), channel_id=1, source_target_pairs={{0,8},{8,16},{16,24},{24,32},{32,40},{40,48},{48,56},{56,64},{64,7... | collective-permute-start | bytes 1769480 | tf_op jit(solution)/shard_map/ppermute | solution.py:14
  233.6 127.7 %collective-permute-start.13 = (bf16[384,3,256]{2,0,1:T(8,128)(2,1)}, bf16[384,3,256]{2,0,1:T(8,128)(2,1)}, u32[]{:S(2)}, u32[]{:S(2)}) collective-permute-start(bf16[384,3,256]{2,0,1:T(8,128)(2,1)} %slice.214), channel_id=1, source_target_pairs={{0,16},{8,24},{16,32},{24,40},{32,48},{40,56},{48,64},{56,72},{64,... | collective-permute-start | bytes 1769480 | tf_op jit(solution)/shard_map/ppermute | solution.py:14
  256.8 116.2 %collective-permute-start.14 = (bf16[384,3,256]{2,0,1:T(8,128)(2,1)}, bf16[384,3,256]{2,0,1:T(8,128)(2,1)}, u32[]{:S(2)}, u32[]{:S(2)}) collective-permute-start(bf16[384,3,256]{2,0,1:T(8,128)(2,1)} %slice.214), channel_id=1, source_target_pairs={{0,24},{8,32},{16,40},{24,48},{32,56},{40,64},{48,72},{56,80},{64,... | collective-permute-start | bytes 1769480 | tf_op jit(solution)/shard_map/ppermute | solution.py:14
  284.5 90.4 %collective-permute-start.15 = (bf16[384,3,256]{2,0,1:T(8,128)(2,1)}, bf16[384,3,256]{2,0,1:T(8,128)(2,1)}, u32[]{:S(2)}, u32[]{:S(2)}) collective-permute-start(bf16[384,3,256]{2,0,1:T(8,128)(2,1)} %slice.214), channel_id=1, source_target_pairs={{0,32},{8,40},{16,48},{24,56},{32,64},{40,72},{48,80},{56,88},{64,... | collective-permute-start | bytes 1769480 | tf_op jit(solution)/shard_map/ppermute | solution.py:14
  328.6 48.2 %collective-permute-start.16 = (bf16[384,3,256]{2,0,1:T(8,128)(2,1)}, bf16[384,3,256]{2,0,1:T(8,128)(2,1)}, u32[]{:S(2)}, u32[]{:S(2)}) collective-permute-start(bf16[384,3,256]{2,0,1:T(8,128)(2,1)} %slice.214), channel_id=1, source_target_pairs={{0,40},{8,48},{16,56},{24,64},{32,72},{40,80},{48,88},{56,96},{64,... | collective-permute-start | bytes 1769480 | tf_op jit(solution)/shard_map/ppermute | solution.py:14
  330.6 66.9 %collective-permute-start.17 = (bf16[384,3,256]{2,0,1:T(8,128)(2,1)}, bf16[384,3,256]{2,0,1:T(8,128)(2,1)}, u32[]{:S(2)}, u32[]{:S(2)}) collective-permute-start(bf16[384,3,256]{2,0,1:T(8,128)(2,1)} %slice.214), channel_id=1, source_target_pairs={{0,48},{8,56},{16,64},{24,72},{32,80},{40,88},{48,96},{56,104},{64... | collective-permute-start | bytes 1769480 | tf_op jit(solution)/shard_map/ppermute | solution.py:14
  361.3 69.0 %collective-permute-start.18 = (bf16[384,3,256]{2,0,1:T(8,128)(2,1)}, bf16[384,3,256]{2,0,1:T(8,128)(2,1)}, u32[]{:S(2)}, u32[]{:S(2)}) collective-permute-start(bf16[384,3,256]{2,0,1:T(8,128)(2,1)} %slice.214), channel_id=1, source_target_pairs={{0,56},{8,64},{16,72},{24,80},{32,88},{40,96},{48,104},{56,112},{6... | collective-permute-start | bytes 1769480 | tf_op jit(solution)/shard_map/ppermute | solution.py:14
  373.0 208.7 %collective-permute-start.19 = (bf16[384,3,256]{2,0,1:T(8,128)(2,1)}, bf16[384,3,256]{2,0,1:T(8,128)(2,1)}, u32[]{:S(2)}, u32[]{:S(2)}) collective-permute-start(bf16[384,3,256]{2,0,1:T(8,128)(2,1)} %slice.214), channel_id=1, source_target_pairs={{0,64},{8,72},{16,80},{24,88},{32,96},{40,104},{48,112},{56,120},{... | collective-permute-start | bytes 1769480 | tf_op jit(solution)/shard_map/ppermute | solution.py:14
  374.9 212.4 %collective-permute-start.20 = (bf16[384,3,256]{2,0,1:T(8,128)(2,1)}, bf16[384,3,256]{2,0,1:T(8,128)(2,1)}, u32[]{:S(2)}, u32[]{:S(2)}) collective-permute-start(bf16[384,3,256]{2,0,1:T(8,128)(2,1)} %slice.214), channel_id=1, source_target_pairs={{0,72},{8,80},{16,88},{24,96},{32,104},{40,112},{48,120},{56,128},... | collective-permute-start | bytes 1769480 | tf_op jit(solution)/shard_map/ppermute | solution.py:14
  376.9 210.4 %collective-permute-start.21 = (bf16[384,3,256]{2,0,1:T(8,128)(2,1)}, bf16[384,3,256]{2,0,1:T(8,128)(2,1)}, u32[]{:S(2)}, u32[]{:S(2)}) collective-permute-start(bf16[384,3,256]{2,0,1:T(8,128)(2,1)} %slice.214), channel_id=1, source_target_pairs={{0,80},{8,88},{16,96},{24,104},{32,112},{40,120},{48,128},{56,136}... | collective-permute-start | bytes 1769480 | tf_op jit(solution)/shard_map/ppermute | solution.py:14
  397.4 189.9 %collective-permute-start.22 = (bf16[384,3,256]{2,0,1:T(8,128)(2,1)}, bf16[384,3,256]{2,0,1:T(8,128)(2,1)}, u32[]{:S(2)}, u32[]{:S(2)}) collective-permute-start(bf16[384,3,256]{2,0,1:T(8,128)(2,1)} %slice.214), channel_id=1, source_target_pairs={{0,88},{8,96},{16,104},{24,112},{32,120},{40,128},{48,136},{56,144... | collective-permute-start | bytes 1769480 | tf_op jit(solution)/shard_map/ppermute | solution.py:14
  430.4 157.1 %collective-permute-start.23 = (bf16[384,3,256]{2,0,1:T(8,128)(2,1)}, bf16[384,3,256]{2,0,1:T(8,128)(2,1)}, u32[]{:S(2)}, u32[]{:S(2)}) collective-permute-start(bf16[384,3,256]{2,0,1:T(8,128)(2,1)} %slice.214), channel_id=1, source_target_pairs={{0,96},{8,104},{16,112},{24,120},{32,128},{40,136},{48,144},{56,15... | collective-permute-start | bytes 1769480 | tf_op jit(solution)/shard_map/ppermute | solution.py:14
  590.7 59.6 %copy-start.3 = (f32[3072]{0:T(1024)S(1)}, f32[3072]{0:T(1024)}, u32[]{:S(2)}) copy-start(f32[3072]{0:T(1024)} %param.61) | copy-start | bytes 36868
Sparse Core Ops, SparseCore 0:
  590.8 59.3 reduce-scatter.1
